TPU v7x, 256 devices: a whole 4x4x8 slice. The times are simulated.
256 devices in a mesh: dp: 16 (over z, core), vocab: 16 (over x, y).
Axes of the slice: x: 4, y: 4, z: 8, core: 2. Of those that a mesh axis runs over, the one named last changes fastest.
Arguments:
- hidden: bfloat16 [4096, 4096], P('dp')
- table: bfloat16 [16384, 4096], P(('vocab', 'dp')), as said below
- targets: int32 [4096], P('dp'), may hold values from 0 to 16383
- token_scale: float32 [4096], P('dp'), may hold values from 2 to 32
- enc_ids: int32 [4096], P(('dp', 'vocab')), may hold values from 0 to 16383
- enc_cot: bfloat16 [4096, 4096], P(('dp', 'vocab')), may hold values from -6 to 6
- dec_ids: int32 [4096], P(('dp', 'vocab')), may hold values from 0 to 16383
- dec_cot: bfloat16 [4096, 4096], P(('dp', 'vocab')), may hold values from -6 to 6
Outputs:
- grad_hidden: bfloat16 [4096, 4096], P('dp', 'vocab')
- grad_table: float32 [16384, 4096], P(('vocab', 'dp'))
- loss: float32 [4096], P('dp')
Inputs may be any that keep to these rules, and one draw needn't show every extreme that they name: table entries of order 3 / sqrt(4096).
All inputs are finite; a program needn't handle non-finite values.
Results may differ from a plain program's by a relative error of at most 0.018.
Values may be sent and summed in bfloat16 or wider, within the bound.
No kernel may reach another device: no remote copies, remote signals or barrier semaphores. Data moves between devices by JAX's collectives and lax.ppermute only.
A program may use at most 128 MiB of HBM per device.

v0:
```python
import jax
import jax.numpy as jnp
from jax import lax
from jax.sharding import PartitionSpec as P


def shards(hidden, table, targets, token_scale, enc_ids, enc_cot, dec_ids, dec_cot):
    vocab_rows = table.shape[0] * lax.axis_size("dp")
    offset = lax.axis_index("vocab") * vocab_rows
    gathered = lax.all_gather(table, "dp", axis=0, tiled=True)
    logits = jnp.dot(hidden, gathered.T, preferred_element_type=jnp.float32)
    local_target = targets - offset
    columns = jnp.arange(vocab_rows, dtype=jnp.int32)
    matches = columns[None, :] == local_target[:, None]
    target_part = jnp.sum(jnp.where(matches, logits, 0.0), axis=1)
    local_max = jnp.max(logits, axis=1)
    row_max = lax.pmax(local_max, "vocab")
    expo = jnp.exp(logits - row_max[:, None])
    row_sum, target_logit = lax.psum((jnp.sum(expo, axis=1), target_part), "vocab")
    loss = row_max + jnp.log(row_sum) - target_logit
    dlogits = (
        token_scale[:, None] * (expo / row_sum[:, None] - matches.astype(jnp.float32))
    ).astype(jnp.bfloat16)
    state_term = jnp.dot(dlogits, gathered, preferred_element_type=jnp.float32)
    grad_hidden = lax.psum_scatter(
        state_term.astype(jnp.bfloat16), "vocab", scatter_dimension=1, tiled=True
    )
    ids_one, cot_one, ids_two, cot_two = (
        lax.all_gather(enc_ids, "vocab", axis=0, tiled=True),
        lax.all_gather(enc_cot, "vocab", axis=0, tiled=True),
        lax.all_gather(dec_ids, "vocab", axis=0, tiled=True),
        lax.all_gather(dec_cot, "vocab", axis=0, tiled=True),
    )
    all_ids = jnp.concatenate([ids_one, ids_two], axis=0) - offset
    all_cot = jnp.concatenate([cot_one, cot_two], axis=0)
    hits = (columns[:, None] == all_ids[None, :]).astype(jnp.bfloat16)
    looked_up = jnp.dot(hits, all_cot, preferred_element_type=jnp.float32)
    head = lax.dot_general(
        dlogits, hidden, (((0,), (0,)), ((), ())), preferred_element_type=jnp.float32
    )
    grad_table = lax.psum_scatter(
        (head + looked_up).astype(jnp.bfloat16), "dp", scatter_dimension=0, tiled=True
    ).astype(jnp.float32)
    return (grad_hidden, grad_table, loss)


def solution(mesh):
    placed = (
        P("dp", None),
        P(("vocab", "dp"), None),
        P("dp"),
        P("dp"),
        P(("dp", "vocab")),
        P(("dp", "vocab"), None),
        P(("dp", "vocab")),
        P(("dp", "vocab"), None),
    )
    return jax.shard_map(
        shards,
        mesh=mesh,
        in_specs=placed,
        out_specs=(P("dp", "vocab"), P(("vocab", "dp"), None), P("dp")),
        check_vma=False,
    )
```

profile of v0, /device:TPU:32, one launch (start us, length us, event | category | flops | bytes accessed | tf_op | source)
XLA Modules:
  0.0 417.9 jit_solution(18154777926044538096)
XLA Ops:
  7.2 0.0 copy-start
  7.2 0.0 all-gather.6.cloned.1.call-start
  7.2 0.7 all-gather.6.cloned.1.call-update
  7.9 0.0 all-gather.8.cloned.1.call-start
  8.0 0.7 all-gather.8.cloned.1.call-update
  8.7 0.0 all-gather.4.cloned.1.call-start
  8.7 0.7 all-gather.4.cloned.1.call-update
  9.4 0.0 reduce-scatter.5.cloned.1.call-start
  9.4 1.3 dynamic-slice
  11.4 0.9 dynamic-update-slice.1
  12.2 0.8 dynamic-update-slice
  13.1 16.5 %all-reduce.2 = (s32[256]{0:T(256)S(1)}, s32[256]{0:T(256)S(1)}) all-reduce(s32[256]{0:T(256)S(1)} %dynamic-update-slice.1, s32[256]{0:T(256)S(1)} %dynamic-update-slice), channel_id=1, replica_groups=mesh['dp'=16,'vocab'=16] {'vocab'}, use_global_device_ids=true, to_apply=%add.1 | all-reduce | flops 512 | bytes 4096
  29.5 0.7 broadcast_subtract_fusion
  30.2 32.8 %all-gather.6.cloned.1.call-done = bf16[256,4096]{1,0:T(8,128)(2,1)} async-done(((bf16[16,4096]{1,0:T(8,128)(2,1)}), bf16[256,4096]{1,0:T(8,128)(2,1)}) %all-gather.6.cloned.1.call-update) | async-done | bytes 2097168 | tf_op jit(solution)/shard_map/all_gather | solution.py:30
  63.0 51.8 %all-gather.8.cloned.1.call-done = bf16[256,4096]{1,0:T(8,128)(2,1)} async-done(((bf16[16,4096]{1,0:T(8,128)(2,1)}), bf16[256,4096]{1,0:T(8,128)(2,1)}) %all-gather.8.cloned.1.call-update) | async-done | bytes 2097168 | tf_op jit(solution)/shard_map/all_gather | solution.py:32
  114.8 10.3 %fusion = f32[1024,4096]{1,0:T(8,128)} fusion(bf16[256,4096]{1,0:T(8,128)(2,1)} %all-gather.8.cloned.1.call-done, bf16[256,4096]{1,0:T(8,128)(2,1)} %all-gather.6.cloned.1.call-done, s32[512]{0:T(512)S(1)} %add_subtract_fusion), kind=kOutput, calls=%fused_computation.2 | convolution fusion | flops 4303880192 | bytes 20973568 | tf_op jit(solution)/shard_map/dot_general | solution.py:37
  125.1 0.0 copy-start.1
  125.1 45.1 %all-gather.4.cloned.1.call-done = bf16[1024,4096]{1,0:T(8,128)(2,1)} async-done(((bf16[64,4096]{1,0:T(8,128)(2,1)}), bf16[1024,4096]{1,0:T(8,128)(2,1)}) %all-gather.4.cloned.1.call-update) | async-done | bytes 8388624 | tf_op jit(solution)/shard_map/all_gather | solution.py:10
  170.2 0.0 copy-done
  170.2 5.8 %fusion.7 = (f32[256]{0:T(256)S(1)}, f32[256,1024]{1,0:T(8,128)S(1)}) fusion(bf16[256,4096]{1,0:T(8,128)(2,1)S(1)} %copy-done, bf16[1024,4096]{1,0:T(8,128)(2,1)} %all-gather.4.cloned.1.call-done), kind=kOutput, calls=%fused_computation.17 | convolution fusion | flops 2147745536 | bytes 11535360 | tf_op jit(solution)/shard_map/dot_general | solution.py:11
  176.0 40.3 %pmax.7 = f32[256]{0:T(256)S(1)} all-reduce(f32[256]{0:T(256)S(1)} %get-tuple-element.9), channel_id=1, replica_groups=mesh['dp'=16,'vocab'=16] {'vocab'}, use_global_device_ids=true, to_apply=%region_1.2 | all-reduce | flops 256 | bytes 2048 | tf_op jit(solution)/shard_map/pmax | solution.py:17
  216.4 0.5 select_reduce_fusion
  216.8 35.5 %all-reduce.3 = (f32[256]{0:T(256)S(1)}, f32[256]{0:T(256)S(1)}) all-reduce(f32[256]{0:T(256)S(1)} %get-tuple-element.4, f32[256]{0:T(256)S(1)} %get-tuple-element.3), channel_id=1, replica_groups=mesh['dp'=16,'vocab'=16] {'vocab'}, use_global_device_ids=true, to_apply=%region_3.4 | all-reduce | flops 512 | bytes 4096 | tf_op jit(solution)/shard_map/psum | solution.py:19
  252.3 0.0 copy-done.1
  252.3 9.2 %add_convert_fusion = bf16[1024,4096]{1,0:T(8,128)(2,1)} fusion(f32[1024,4096]{1,0:T(8,128)} %fusion, bf16[256,4096]{1,0:T(8,128)(2,1)S(1)} %copy-done, f32[256,1024]{1,0:T(8,128)S(1)} %get-tuple-element.10, s32[256]{0:T(256)S(1)} %broadcast_subtract_fusion, f32[256]{0:T(256)S(1)} %get-tuple-element.7, f32[256]{0:T(256)S(1)} %pmax.7, f32[256]{0:T(256)S(1)} %copy-done.1), kind=kOutput, calls=%fused_computation | convolution fusion | flops 2157707264 | bytes 28315648 | tf_op jit(solution)/shard_map/dot_general | solution.py:38
  261.5 0.0 reduce-scatter.5.cloned.1.call-update
  261.5 0.0 reduce-scatter.3.cloned.1.call-start
  261.6 7.4 %convolution_convert_fusion = bf16[256,4096]{1,0:T(8,128)(2,1)} fusion(bf16[1024,4096]{1,0:T(8,128)(2,1)} %all-gather.4.cloned.1.call-done, f32[256,1024]{1,0:T(8,128)S(1)} %get-tuple-element.10, s32[256]{0:T(256)S(1)} %broadcast_subtract_fusion, f32[256]{0:T(256)S(1)} %get-tuple-element.7, f32[256]{0:T(256)S(1)} %pmax.7, f32[256]{0:T(256)S(1)} %copy-done.1), kind=kOutput, calls=%fused_computation.1 | convolution fusion | flops 2150367232 | bytes 11538432 | tf_op jit(solution)/shard_map/dot_general | solution.py:24
  268.9 0.0 reduce-scatter.3.cloned.1.call-update
  269.0 0.6 add_subtract_fusion.1
  269.5 56.1 %reduce-scatter.5.cloned.1.call-done = bf16[64,4096]{1,0:T(8,128)(2,1)} async-done(((bf16[1024,4096]{1,0:T(8,128)(2,1)}), bf16[64,4096]{1,0:T(8,128)(2,1)}) %reduce-scatter.5.cloned.1.call-update) | async-done | bytes 524304 | tf_op jit(solution)/shard_map/reduce_scatter | solution.py:41
  325.6 2.1 convert_element_type.20
  327.7 83.7 %reduce-scatter.3.cloned.1.call-done = bf16[256,256]{1,0:T(8,128)(2,1)} async-done(((bf16[256,4096]{1,0:T(8,128)(2,1)}), bf16[256,256]{1,0:T(8,128)(2,1)}) %reduce-scatter.3.cloned.1.call-update) | async-done | bytes 131088 | tf_op jit(solution)/shard_map/reduce_scatter | solution.py:25
  (3 shorter events, 0.0 us)
Async XLA Ops:
  7.2 163.1 %copy-start = (bf16[256,4096]{1,0:T(8,128)(2,1)S(1)}, bf16[256,4096]{1,0:T(8,128)(2,1)}, u32[]{:S(2)}) copy-start(bf16[256,4096]{1,0:T(8,128)(2,1)} %param.8) | copy-start | bytes 6291460
  7.2 55.8 %all-gather.6.cloned.1.call-start = ((), (), s32[]{:S(2)}) async-start(), calls=%async_computation.4 | async-start | bytes 2228224 | tf_op jit(solution)/shard_map/all_gather | solution.py:30
  7.9 106.9 %all-gather.8.cloned.1.call-start = ((), (), s32[]{:S(2)}) async-start(), calls=%async_computation.5 | async-start | bytes 2228224 | tf_op jit(solution)/shard_map/all_gather | solution.py:32
  8.7 161.5 %all-gather.4.cloned.1.call-start = ((), (), s32[]{:S(2)}) async-start(), calls=%async_computation.2 | async-start | bytes 8912896 | tf_op jit(solution)/shard_map/all_gather | solution.py:10
  9.4 316.2 %reduce-scatter.5.cloned.1.call-start = ((), (), s32[]{:S(2)}) async-start(), calls=%async_computation.6 | async-start | bytes 8912896 | tf_op jit(solution)/shard_map/reduce_scatter | solution.py:41
  125.1 127.2 %copy-start.1 = (f32[256]{0:T(256)S(1)}, f32[256]{0:T(256)}, u32[]{:S(2)}) copy-start(f32[256]{0:T(256)} %param.11) | copy-start | bytes 3076
  261.5 149.9 %reduce-scatter.3.cloned.1.call-start = ((), (), s32[]{:S(2)}) async-start(), calls=%async_computation.3 | async-start | bytes 2228224 | tf_op jit(solution)/shard_map/reduce_scatter | solution.py:25
Sparse Core Ops, SparseCore 0:
  10.4 52.5 all-gather.5
  65.5 49.3 all-gather.7
  116.7 53.4 all-gather.3
  261.6 63.9 reduce-scatter.4
  329.6 81.7 reduce-scatter.2
where the time goes:
time: 418 us
  waiting for transfers between devices  272 us (65%)
  blocking collectives  92.2 us (22%)
  matrix products  32.7 us (8%)
  between operations  14.5 us (3%)
    reduce_scatter x1, waiting for transfers between devices, shards(): lax.psum_scatter(state_term.astype(jnp.bfloat16), 'vocab', scatter_dimens...  83.7 us
    reduce_scatter x1, waiting for transfers between devices, shards(): lax.psum_scatter((head + looked_up).astype(jnp.bfloat16), 'dp', scatter_d...  56.1 us
    all_gather x1, waiting for transfers between devices, shards(): lax.all_gather(dec_cot, 'vocab', axis=0, tiled=True)  51.8 us
    all_gather x1, waiting for transfers between devices, shards(): gathered = lax.all_gather(table, 'dp', axis=0, tiled=True)  45.1 us
    pmax x1, blocking collectives, shards(): row_max = lax.pmax(local_max, 'vocab')  40.3 us
    psum x1, blocking collectives, shards(): lax.psum((jnp.sum(expo, axis=1), target_part), 'vocab')  35.5 us
    all_gather x1, waiting for transfers between devices, shards(): lax.all_gather(enc_cot, 'vocab', axis=0, tiled=True)  32.8 us
    unnamed x1, blocking collectives  16.5 us
  transfers between devices with their start and end apart: 5, of which 5 were waited for; matrix products, arithmetic and copies ran while one was open for 6% of the time, Pallas kernels for 0%

commit v1 on v0

--- a/solution.py
+++ b/solution.py
@@ -4,10 +4,31 @@
 from jax.sharding import PartitionSpec as P
 
 
+def gather_around(x, axis, dim):
+    length, position, span = (lax.axis_size(axis), lax.axis_index(axis), x.shape[dim])
+    ahead = [(i, (i + 1) % length) for i in range(length)]
+    left = [(i, (i - 1) % length) for i in range(length)]
+    filled = jnp.zeros((*x.shape[:dim], length * span, *x.shape[dim + 1 :]), x.dtype)
+    filled = lax.dynamic_update_slice_in_dim(filled, x, position * span, axis=dim)
+    from_left = from_right = x
+    half = length // 2
+    for step in range(1, half + 1):
+        from_left = lax.ppermute(from_left, axis, ahead)
+        filled = lax.dynamic_update_slice_in_dim(
+            filled, from_left, (position - step) % length * span, axis=dim
+        )
+        if step < length - half:
+            from_right = lax.ppermute(from_right, axis, left)
+            filled = lax.dynamic_update_slice_in_dim(
+                filled, from_right, (position + step) % length * span, axis=dim
+            )
+    return filled
+
+
 def shards(hidden, table, targets, token_scale, enc_ids, enc_cot, dec_ids, dec_cot):
     vocab_rows = table.shape[0] * lax.axis_size("dp")
     offset = lax.axis_index("vocab") * vocab_rows
-    gathered = lax.all_gather(table, "dp", axis=0, tiled=True)
+    gathered = gather_around(table, "dp", 0)
     logits = jnp.dot(hidden, gathered.T, preferred_element_type=jnp.float32)
     local_target = targets - offset
     columns = jnp.arange(vocab_rows, dtype=jnp.int32)

time: 418 us -> 375 us (0.90)
  waiting for transfers between devices: 272 us -> 195 us
  local copies, waits for them, and re-layouts: 2.98 us -> 21.8 us
  starting transfers between devices: 0.19 us -> 14.6 us
    all_gather x1, waiting for transfers between devices: 51.8 us -> 0.01 us  [shards(): lax.all_gather(dec_cot, 'vocab', axis=0, tiled=True)]
    all_gather x1 -> x0, waiting for transfers between devices: 45.1 us -> none  [shards(): gathered = lax.all_gather(table, 'dp', axis=0, tiled=True)]
    ppermute x0 -> x15, waiting for transfers between devices: none -> 28.6 us  [the longest x8 26.5 us: gather_around(): from_left = lax.ppermute(from_left, axis, ahead)]
    dynamic_update_slice x0 -> x16, local copies, waits for them, and re-layouts: none -> 14.6 us  [the longest x8 7.82 us: gather_around(): lax.dynamic_update_slice_in_dim(filled, from_left, (position - step) % le...]
    ppermute x0 -> x15, starting transfers between devices: none -> 14.3 us  [the longest x7 14.2 us: gather_around(): from_right = lax.ppermute(from_right, axis, left)]
    all_gather x1, waiting for transfers between devices: 32.8 us -> 24.8 us  [shards(): lax.all_gather(enc_cot, 'vocab', axis=0, tiled=True)]
    broadcast_in_dim x0 -> x1, local copies, waits for them, and re-layouts: none -> 4.27 us  [gather_around(): jnp.zeros((*x.shape[:dim], length * span, *x.shape[dim + 1:]), x.dtype)]
  transfers between devices with their start and end apart: 5 -> 19, of which waited for: 5 -> 13; matrix products, arithmetic and copies ran while one was open for 6% -> 11% of each run, Pallas kernels for 0% -> 0%
where the time goes in v1:
time: 375 us
  waiting for transfers between devices  195 us (52%)
  blocking collectives  90 us (24%)
  matrix products  34.8 us (9%)
  local copies, waits for them, and re-layouts  21.8 us (6%)
  between operations  14.8 us (4%)
  starting transfers between devices  14.6 us (4%)
    reduce_scatter x1, waiting for transfers between devices, shards(): lax.psum_scatter(state_term.astype(jnp.bfloat16), 'vocab', scatter_dimens...  83.8 us
    reduce_scatter x1, waiting for transfers between devices, shards(): lax.psum_scatter((head + looked_up).astype(jnp.bfloat16), 'dp', scatter_d...  56.9 us
    pmax x1, blocking collectives, shards(): row_max = lax.pmax(local_max, 'vocab')  38.1 us
    psum x1, blocking collectives, shards(): lax.psum((jnp.sum(expo, axis=1), target_part), 'vocab')  35.5 us
    ppermute x8, waiting for transfers between devices, gather_around(): from_left = lax.ppermute(from_left, axis, ahead)  26.5 us
    all_gather x1, waiting for transfers between devices, shards(): lax.all_gather(enc_cot, 'vocab', axis=0, tiled=True)  24.8 us
    unnamed x1, blocking collectives  16.5 us
    ppermute x7, starting transfers between devices, gather_around(): from_right = lax.ppermute(from_right, axis, left)  14.2 us
  transfers between devices with their start and end apart: 19, of which 13 were waited for; matrix products, arithmetic and copies ran while one was open for 11% of the time, Pallas kernels for 0%

profile of v1, /device:TPU:32, one launch (start us, length us, event | category | flops | bytes accessed | tf_op | source)
XLA Modules:
  0.0 374.6 jit_solution(12719598059215462117)
XLA Ops:
  7.2 0.0 copy-start
  7.2 0.0 all-gather.5.cloned.1.call-start
  7.2 0.7 all-gather.5.cloned.1.call-update
  7.9 0.0 all-gather.3.cloned.1.call-start
  8.0 0.0 collective-permute-start
  8.0 1.7 collective-permute-start.1
  9.7 0.0 all-gather.3.cloned.1.call-update
  9.8 0.0 reduce-scatter.5.cloned.1.call-start
  10.1 0.7 broadcast_subtract_fusion
  10.8 1.3 dynamic-slice
  12.7 0.9 dynamic-update-slice.1
  13.6 0.8 dynamic-update-slice
  14.4 16.5 %all-reduce.2 = (s32[256]{0:T(256)S(1)}, s32[256]{0:T(256)S(1)}) all-reduce(s32[256]{0:T(256)S(1)} %dynamic-update-slice.1, s32[256]{0:T(256)S(1)} %dynamic-update-slice), channel_id=1, replica_groups=mesh['dp'=16,'vocab'=16] {'vocab'}, use_global_device_ids=true, to_apply=%add.1 | all-reduce | flops 512 | bytes 4096
  30.9 4.3 %broadcast_in_dim.6 = bf16[1024,4096]{1,0:T(8,128)(2,1)} broadcast(bf16[]{:T(256)} %constant.93.clone.1), dimensions={} | broadcast | bytes 8388610 | tf_op jit(solution)/shard_map/broadcast_in_dim | solution.py:11
  35.2 0.8 constant_dynamic-update-slice_fusion.15
  36.0 0.0 collective-permute-done.1
  36.0 1.7 collective-permute-start.3
  37.8 1.9 constant_dynamic-update-slice_fusion.14
  39.7 0.8 constant_dynamic-update-slice_fusion.13
  40.5 4.3 %collective-permute-done.2 = bf16[64,4096]{1,0:T(8,128)(2,1)S(1)} collective-permute-done((bf16[64,4096]{1,0:T(8,128)(2,1)}, bf16[64,4096]{1,0:T(8,128)(2,1)S(1)}, u32[]{:S(2)}, u32[]{:S(2)}) %collective-permute-start.2) | collective-permute-done | bytes 524320 | tf_op jit(solution)/shard_map/ppermute | solution.py:16
  44.8 0.0 collective-permute-start.4
  44.8 1.8 collective-permute-start.5
  46.7 0.9 constant_dynamic-update-slice_fusion.12
  47.5 0.8 constant_dynamic-update-slice_fusion.11
  48.4 5.1 %collective-permute-done.4 = bf16[64,4096]{1,0:T(8,128)(2,1)S(1)} collective-permute-done((bf16[64,4096]{1,0:T(8,128)(2,1)S(1)}, bf16[64,4096]{1,0:T(8,128)(2,1)S(1)}, u32[]{:S(2)}, u32[]{:S(2)}) %collective-permute-start.4) | collective-permute-done | bytes 524320 | tf_op jit(solution)/shard_map/ppermute | solution.py:16
  53.4 0.0 collective-permute-start.6
  53.4 2.2 collective-permute-start.7
  55.7 0.9 constant_dynamic-update-slice_fusion.10
  56.5 0.8 constant_dynamic-update-slice_fusion.9
  57.4 4.7 %collective-permute-done.6 = bf16[64,4096]{1,0:T(8,128)(2,1)S(1)} collective-permute-done((bf16[64,4096]{1,0:T(8,128)(2,1)S(1)}, bf16[64,4096]{1,0:T(8,128)(2,1)S(1)}, u32[]{:S(2)}, u32[]{:S(2)}) %collective-permute-start.6) | collective-permute-done | bytes 524320 | tf_op jit(solution)/shard_map/ppermute | solution.py:16
  62.1 0.3 collective-permute-done.7
  62.4 2.2 collective-permute-start.9
  64.6 0.9 constant_dynamic-update-slice_fusion.8
  65.4 0.8 constant_dynamic-update-slice_fusion.7
  66.3 4.4 %collective-permute-done.8 = bf16[64,4096]{1,0:T(8,128)(2,1)S(1)} collective-permute-done((bf16[64,4096]{1,0:T(8,128)(2,1)S(1)}, bf16[64,4096]{1,0:T(8,128)(2,1)S(1)}, u32[]{:S(2)}, u32[]{:S(2)}) %collective-permute-start.8) | collective-permute-done | bytes 524320 | tf_op jit(solution)/shard_map/ppermute | solution.py:16
  70.7 0.6 collective-permute-done.9
  71.3 2.2 collective-permute-start.11
  73.5 0.8 constant_dynamic-update-slice_fusion.6
  74.3 0.8 constant_dynamic-update-slice_fusion.5
  75.2 4.1 %collective-permute-done.10 = bf16[64,4096]{1,0:T(8,128)(2,1)S(1)} collective-permute-done((bf16[64,4096]{1,0:T(8,128)(2,1)S(1)}, bf16[64,4096]{1,0:T(8,128)(2,1)S(1)}, u32[]{:S(2)}, u32[]{:S(2)}) %collective-permute-start.10) | collective-permute-done | bytes 524320 | tf_op jit(solution)/shard_map/ppermute | solution.py:16
  79.3 0.9 collective-permute-done.11
  80.2 2.3 collective-permute-start.13
  82.5 0.8 constant_dynamic-update-slice_fusion.4
  83.3 0.8 constant_dynamic-update-slice_fusion.3
  84.2 3.9 %collective-permute-done.12 = bf16[64,4096]{1,0:T(8,128)(2,1)S(1)} collective-permute-done((bf16[64,4096]{1,0:T(8,128)(2,1)S(1)}, bf16[64,4096]{1,0:T(8,128)(2,1)S(1)}, u32[]{:S(2)}, u32[]{:S(2)}) %collective-permute-start.12) | collective-permute-done | bytes 524320 | tf_op jit(solution)/shard_map/ppermute | solution.py:16
  88.1 0.8 constant_dynamic-update-slice_fusion.2
  88.9 0.3 collective-permute-done.13
  89.2 0.9 constant_dynamic-update-slice_fusion.1
  90.1 24.8 %all-gather.3.cloned.1.call-done = bf16[256,4096]{1,0:T(8,128)(2,1)} async-done(((bf16[16,4096]{1,0:T(8,128)(2,1)}), bf16[256,4096]{1,0:T(8,128)(2,1)}) %all-gather.3.cloned.1.call-update) | async-done | bytes 2097168 | tf_op jit(solution)/shard_map/all_gather | solution.py:51
  114.9 10.3 %fusion = f32[1024,4096]{1,0:T(8,128)} fusion(bf16[256,4096]{1,0:T(8,128)(2,1)} %all-gather.5.cloned.1.call-done, bf16[256,4096]{1,0:T(8,128)(2,1)} %all-gather.3.cloned.1.call-done, s32[512]{0:T(512)S(1)} %add_subtract_fusion), kind=kOutput, calls=%fused_computation.2 | convolution fusion | flops 4303880192 | bytes 20973568 | tf_op jit(solution)/shard_map/dot_general | solution.py:58
  125.2 0.8 constant_dynamic-update-slice_fusion
  126.0 5.8 %fusion.9 = (f32[256]{0:T(256)S(1)}, f32[1024,256]{1,0:T(8,128)S(1)}) fusion(bf16[1024,4096]{1,0:T(8,128)(2,1)} %constant_dynamic-update-slice_fusion, bf16[256,4096]{1,0:T(8,128)(2,1)S(1)} %copy-done), kind=kOutput, calls=%fused_computation.35 | convolution fusion | flops 2147745536 | bytes 11535360 | tf_op jit(solution)/shard_map/dot_general | solution.py:32
  131.8 38.1 %pmax.7 = f32[256]{0:T(256)S(1)} all-reduce(f32[256]{0:T(256)S(1)} %get-tuple-element.9), channel_id=1, replica_groups=mesh['dp'=16,'vocab'=16] {'vocab'}, use_global_device_ids=true, to_apply=%region_1.2 | all-reduce | flops 256 | bytes 2048 | tf_op jit(solution)/shard_map/pmax | solution.py:38
  169.9 0.3 fusion.5
  170.2 35.5 %all-reduce.3 = (f32[256]{0:T(256)S(1)}, f32[256]{0:T(256)S(1)}) all-reduce(f32[256]{0:T(256)S(1)} %get-tuple-element.4, f32[256]{0:T(256)S(1)} %get-tuple-element.3), channel_id=1, replica_groups=mesh['dp'=16,'vocab'=16] {'vocab'}, use_global_device_ids=true, to_apply=%region_3.4 | all-reduce | flops 512 | bytes 4096 | tf_op jit(solution)/shard_map/psum | solution.py:40
  205.7 11.5 %add_convert_fusion = bf16[1024,4096]{1,0:T(8,128)(2,1)} fusion(f32[1024,4096]{1,0:T(8,128)} %fusion, bf16[256,4096]{1,0:T(8,128)(2,1)S(1)} %copy-done, f32[1024,256]{1,0:T(8,128)S(1)} %get-tuple-element.10, s32[256]{0:T(256)S(1)} %broadcast_subtract_fusion, f32[256]{0:T(256)S(1)} %get-tuple-element.7, f32[256]{0:T(256)S(1)} %pmax.7, f32[256]{0:T(256)S(1)} %copy-done.2), kind=kOutput, calls=%fused_computation | convolution fusion | flops 2157707264 | bytes 28315648 | tf_op jit(solution)/shard_map/dot_general | solution.py:59
  217.2 0.0 reduce-scatter.5.cloned.1.call-update
  217.2 0.2 reduce-scatter.3.cloned.1.call-start
  217.4 7.2 %convolution_convert_fusion = bf16[256,4096]{1,0:T(8,128)(2,1)} fusion(bf16[1024,4096]{1,0:T(8,128)(2,1)} %constant_dynamic-update-slice_fusion, f32[1024,256]{1,0:T(8,128)S(1)} %get-tuple-element.10, s32[256]{0:T(256)S(1)} %broadcast_subtract_fusion, f32[256]{0:T(256)S(1)} %get-tuple-element.7, f32[256]{0:T(256)S(1)} %pmax.7, f32[256]{0:T(256)S(1)} %copy-done.2), kind=kOutput, calls=%fused_computation.1 | convolution fusion | flops 2150367232 | bytes 11538432 | tf_op jit(solution)/shard_map/dot_general | solution.py:45
  224.6 0.0 reduce-scatter.3.cloned.1.call-update
  224.7 0.6 add_subtract_fusion.1
  225.2 56.9 %reduce-scatter.5.cloned.1.call-done = bf16[64,4096]{1,0:T(8,128)(2,1)} async-done(((bf16[1024,4096]{1,0:T(8,128)(2,1)}), bf16[64,4096]{1,0:T(8,128)(2,1)}) %reduce-scatter.5.cloned.1.call-update) | async-done | bytes 524304 | tf_op jit(solution)/shard_map/reduce_scatter | solution.py:62
  282.2 2.1 convert_element_type.20
  284.3 83.8 %reduce-scatter.3.cloned.1.call-done = bf16[256,256]{1,0:T(8,128)(2,1)} async-done(((bf16[256,4096]{1,0:T(8,128)(2,1)}), bf16[256,256]{1,0:T(8,128)(2,1)}) %reduce-scatter.3.cloned.1.call-update) | async-done | bytes 131088 | tf_op jit(solution)/shard_map/reduce_scatter | solution.py:46
  (18 shorter events, 0.1 us)
Async XLA Ops:
  7.2 118.8 %copy-start = (bf16[256,4096]{1,0:T(8,128)(2,1)S(1)}, bf16[256,4096]{1,0:T(8,128)(2,1)}, u32[]{:S(2)}) copy-start(bf16[256,4096]{1,0:T(8,128)(2,1)} %param.8) | copy-start | bytes 6291460
  7.2 28.0 %copy-start.1 = (bf16[64,4096]{1,0:T(8,128)(2,1)S(1)}, bf16[64,4096]{1,0:T(8,128)(2,1)}, u32[]{:S(2)}) copy-start(bf16[64,4096]{1,0:T(8,128)(2,1)} %param.9) | copy-start | bytes 1572868
  7.2 82.9 %all-gather.5.cloned.1.call-start = ((), (), s32[]{:S(2)}) async-start(), calls=%async_computation.4 | async-start | bytes 2228224 | tf_op jit(solution)/shard_map/all_gather | solution.py:53
  7.9 106.9 %all-gather.3.cloned.1.call-start = ((), (), s32[]{:S(2)}) async-start(), calls=%async_computation.3 | async-start | bytes 2228224 | tf_op jit(solution)/shard_map/all_gather | solution.py:51
  8.0 28.0 %collective-permute-start = (bf16[64,4096]{1,0:T(8,128)(2,1)}, bf16[64,4096]{1,0:T(8,128)(2,1)}, u32[]{:S(2)}, u32[]{:S(2)}) collective-permute-start(bf16[64,4096]{1,0:T(8,128)(2,1)} %param.9), channel_id=1, source_target_pairs={{0,16},{16,32},{32,48},{48,64},{64,80},{80,96},{96,112},{112,128},... | collective-permute-start | bytes 1572872 | tf_op jit(solution)/shard_map/ppermute | solution.py:16
  8.0 28.0 %collective-permute-start.1 = (bf16[64,4096]{1,0:T(8,128)(2,1)}, bf16[64,4096]{1,0:T(8,128)(2,1)S(1)}, u32[]{:S(2)}, u32[]{:S(2)}) collective-permute-start(bf16[64,4096]{1,0:T(8,128)(2,1)} %param.9), channel_id=1, source_target_pairs={{0,240},{16,0},{32,16},{48,32},{64,48},{80,64},{96,80},{112,96},{1... | collective-permute-start | bytes 1572872 | tf_op jit(solution)/shard_map/ppermute | solution.py:21
  9.8 272.4 %reduce-scatter.5.cloned.1.call-start = ((), (), s32[]{:S(2)}) async-start(), calls=%async_computation.5 | async-start | bytes 8912896 | tf_op jit(solution)/shard_map/reduce_scatter | solution.py:62
  36.0 8.8 %collective-permute-start.2 = (bf16[64,4096]{1,0:T(8,128)(2,1)}, bf16[64,4096]{1,0:T(8,128)(2,1)S(1)}, u32[]{:S(2)}, u32[]{:S(2)}) collective-permute-start(bf16[64,4096]{1,0:T(8,128)(2,1)} %collective-permute-done), channel_id=1, source_target_pairs={{0,16},{16,32},{32,48},{48,64},{64,80},{80,96},{96,112},{112,128},... | collective-permute-start | bytes 1572872 | tf_op jit(solution)/shard_map/ppermute | solution.py:16
  36.0 8.8 %collective-permute-start.3 = (bf16[64,4096]{1,0:T(8,128)(2,1)S(1)}, bf16[64,4096]{1,0:T(8,128)(2,1)S(1)}, u32[]{:S(2)}, u32[]{:S(2)}) collective-permute-start(bf16[64,4096]{1,0:T(8,128)(2,1)S(1)} %collective-permute-done.1), channel_id=1, source_target_pairs={{0,240},{16,0},{32,16},{48,32},{64,48},{80,64},{96,80},{112,96},{1... | collective-permute-start | bytes 1572872 | tf_op jit(solution)/shard_map/ppermute | solution.py:21
  44.8 8.6 %collective-permute-start.4 = (bf16[64,4096]{1,0:T(8,128)(2,1)S(1)}, bf16[64,4096]{1,0:T(8,128)(2,1)S(1)}, u32[]{:S(2)}, u32[]{:S(2)}) collective-permute-start(bf16[64,4096]{1,0:T(8,128)(2,1)S(1)} %collective-permute-done.2), channel_id=1, source_target_pairs={{0,16},{16,32},{32,48},{48,64},{64,80},{80,96},{96,112},{112,128},... | collective-permute-start | bytes 1572872 | tf_op jit(solution)/shard_map/ppermute | solution.py:16
  44.8 8.6 %collective-permute-start.5 = (bf16[64,4096]{1,0:T(8,128)(2,1)S(1)}, bf16[64,4096]{1,0:T(8,128)(2,1)S(1)}, u32[]{:S(2)}, u32[]{:S(2)}) collective-permute-start(bf16[64,4096]{1,0:T(8,128)(2,1)S(1)} %collective-permute-done.3), channel_id=1, source_target_pairs={{0,240},{16,0},{32,16},{48,32},{64,48},{80,64},{96,80},{112,96},{1... | collective-permute-start | bytes 1572872 | tf_op jit(solution)/shard_map/ppermute | solution.py:21
  53.4 8.6 %collective-permute-start.6 = (bf16[64,4096]{1,0:T(8,128)(2,1)S(1)}, bf16[64,4096]{1,0:T(8,128)(2,1)S(1)}, u32[]{:S(2)}, u32[]{:S(2)}) collective-permute-start(bf16[64,4096]{1,0:T(8,128)(2,1)S(1)} %collective-permute-done.4), channel_id=1, source_target_pairs={{0,16},{16,32},{32,48},{48,64},{64,80},{80,96},{96,112},{112,128},... | collective-permute-start | bytes 1572872 | tf_op jit(solution)/shard_map/ppermute | solution.py:16
  53.4 8.9 %collective-permute-start.7 = (bf16[64,4096]{1,0:T(8,128)(2,1)S(1)}, bf16[64,4096]{1,0:T(8,128)(2,1)S(1)}, u32[]{:S(2)}, u32[]{:S(2)}) collective-permute-start(bf16[64,4096]{1,0:T(8,128)(2,1)S(1)} %collective-permute-done.5), channel_id=1, source_target_pairs={{0,240},{16,0},{32,16},{48,32},{64,48},{80,64},{96,80},{112,96},{1... | collective-permute-start | bytes 1572872 | tf_op jit(solution)/shard_map/ppermute | solution.py:21
  62.0 8.6 %collective-permute-start.8 = (bf16[64,4096]{1,0:T(8,128)(2,1)S(1)}, bf16[64,4096]{1,0:T(8,128)(2,1)S(1)}, u32[]{:S(2)}, u32[]{:S(2)}) collective-permute-start(bf16[64,4096]{1,0:T(8,128)(2,1)S(1)} %collective-permute-done.6), channel_id=1, source_target_pairs={{0,16},{16,32},{32,48},{48,64},{64,80},{80,96},{96,112},{112,128},... | collective-permute-start | bytes 1572872 | tf_op jit(solution)/shard_map/ppermute | solution.py:16
  62.4 8.9 %collective-permute-start.9 = (bf16[64,4096]{1,0:T(8,128)(2,1)S(1)}, bf16[64,4096]{1,0:T(8,128)(2,1)S(1)}, u32[]{:S(2)}, u32[]{:S(2)}) collective-permute-start(bf16[64,4096]{1,0:T(8,128)(2,1)S(1)} %collective-permute-done.7), channel_id=1, source_target_pairs={{0,240},{16,0},{32,16},{48,32},{64,48},{80,64},{96,80},{112,96},{1... | collective-permute-start | bytes 1572872 | tf_op jit(solution)/shard_map/ppermute | solution.py:21
  70.7 8.6 %collective-permute-start.10 = (bf16[64,4096]{1,0:T(8,128)(2,1)S(1)}, bf16[64,4096]{1,0:T(8,128)(2,1)S(1)}, u32[]{:S(2)}, u32[]{:S(2)}) collective-permute-start(bf16[64,4096]{1,0:T(8,128)(2,1)S(1)} %collective-permute-done.8), channel_id=1, source_target_pairs={{0,16},{16,32},{32,48},{48,64},{64,80},{80,96},{96,112},{112,128},... | collective-permute-start | bytes 1572872 | tf_op jit(solution)/shard_map/ppermute | solution.py:16
  71.3 8.9 %collective-permute-start.11 = (bf16[64,4096]{1,0:T(8,128)(2,1)S(1)}, bf16[64,4096]{1,0:T(8,128)(2,1)S(1)}, u32[]{:S(2)}, u32[]{:S(2)}) collective-permute-start(bf16[64,4096]{1,0:T(8,128)(2,1)S(1)} %collective-permute-done.9), channel_id=1, source_target_pairs={{0,240},{16,0},{32,16},{48,32},{64,48},{80,64},{96,80},{112,96},{1... | collective-permute-start | bytes 1572872 | tf_op jit(solution)/shard_map/ppermute | solution.py:21
  79.3 8.8 %collective-permute-start.12 = (bf16[64,4096]{1,0:T(8,128)(2,1)S(1)}, bf16[64,4096]{1,0:T(8,128)(2,1)S(1)}, u32[]{:S(2)}, u32[]{:S(2)}) collective-permute-start(bf16[64,4096]{1,0:T(8,128)(2,1)S(1)} %collective-permute-done.10), channel_id=1, source_target_pairs={{0,16},{16,32},{32,48},{48,64},{64,80},{80,96},{96,112},{112,128},... | collective-permute-start | bytes 1572872 | tf_op jit(solution)/shard_map/ppermute | solution.py:16
  80.2 9.0 %collective-permute-start.13 = (bf16[64,4096]{1,0:T(8,128)(2,1)S(1)}, bf16[64,4096]{1,0:T(8,128)(2,1)S(1)}, u32[]{:S(2)}, u32[]{:S(2)}) collective-permute-start(bf16[64,4096]{1,0:T(8,128)(2,1)S(1)} %collective-permute-done.11), channel_id=1, source_target_pairs={{0,240},{16,0},{32,16},{48,32},{64,48},{80,64},{96,80},{112,96},{1... | collective-permute-start | bytes 1572872 | tf_op jit(solution)/shard_map/ppermute | solution.py:21
  88.1 37.1 %collective-permute-start.14 = (bf16[64,4096]{1,0:T(8,128)(2,1)S(1)}, bf16[64,4096]{1,0:T(8,128)(2,1)S(1)}, u32[]{:S(2)}, u32[]{:S(2)}) collective-permute-start(bf16[64,4096]{1,0:T(8,128)(2,1)S(1)} %collective-permute-done.12), channel_id=1, source_target_pairs={{0,16},{16,32},{32,48},{48,64},{64,80},{80,96},{96,112},{112,128},... | collective-permute-start | bytes 1572872 | tf_op jit(solution)/shard_map/ppermute | solution.py:16
  126.0 79.7 %copy-start.2 = (f32[256]{0:T(256)S(1)}, f32[256]{0:T(256)}, u32[]{:S(2)}) copy-start(f32[256]{0:T(256)} %param.11) | copy-start | bytes 3076
  217.2 150.9 %reduce-scatter.3.cloned.1.call-start = ((), (), s32[]{:S(2)}) async-start(), calls=%async_computation.2 | async-start | bytes 2228224 | tf_op jit(solution)/shard_map/reduce_scatter | solution.py:46
Sparse Core Ops, SparseCore 0:
  10.5 52.5 all-gather.4
  65.5 49.3 all-gather.2
  217.3 64.8 reduce-scatter.4
  286.2 81.8 reduce-scatter.2
